TPU v7x, 32 devices: a whole 2x2x4 slice. The times are simulated.
32 devices in a mesh: section: 16 (over z, y, core), dp: 2 (over x).
Axes of the slice: x: 2, y: 2, z: 4, core: 2. Of those that a mesh axis runs over, the one named last changes fastest.
Arguments:
- activations: bfloat16 [16, 16, 64, 4096], P('section', 'dp'), may hold values from -6 to 6
- out_grads: bfloat16 [16, 16, 64, 4096], P('section', 'dp'), may hold values from -6 to 6
- proj_in: bfloat16 [16, 2, 4096, 128], P('section'), may hold values from -0.09375 to 0.09375
- proj_out: bfloat16 [16, 2, 64, 4096], P('section'), may hold values from -0.09375 to 0.09375
- earlier_gram: float32 [8192, 8192], P('section', 'dp'), may hold values from -4 to 4, as said below
Outputs:
- gram: float32 [8192, 8192], P('section', 'dp')
Inputs may be any that keep to these rules, and one draw needn't show every extreme that they name: earlier_gram is symmetric.
All inputs are finite; a program needn't handle non-finite values.
Results may differ from a plain program's by a relative error of at most 0.0013.
Values sent between devices are 32-bit elements; how exact they have to be, the bound alone decides.
A program may use at most 64 MiB of HBM per device.

v0:
```python
import math
import jax
import jax.numpy as jnp
from jax import lax
from jax.sharding import PartitionSpec as P

PROJ = 2
LEN = 64


def per_device(activations, out_grads, proj_in, proj_out, earlier_gram):
    layer_act = activations[0]
    layer_grad = out_grads[0]
    layer_in = proj_in[0]
    layer_out = proj_out[0]
    low_in = jnp.einsum(
        "etd,pdm->petm", layer_act, layer_in, preferred_element_type=jnp.float32
    ).astype(jnp.bfloat16)
    low_out = jnp.einsum(
        "pkd,etd->pekt", layer_out, layer_grad, preferred_element_type=jnp.float32
    ).astype(jnp.bfloat16)
    partial_terms = jnp.einsum(
        "pekt,petm->ekm", low_out, low_in, preferred_element_type=jnp.float32
    )
    local_count = partial_terms.shape[0]
    partial_terms = partial_terms.reshape(local_count, -1)
    n_layers = lax.axis_size("section")
    n_groups = lax.axis_size("dp")
    total_examples = local_count * n_groups
    scale = 1.0 / math.sqrt(LEN * n_layers * PROJ)
    row_width = earlier_gram.shape[0]
    col_width = earlier_gram.shape[1]
    row_start = lax.axis_index("section") * row_width
    col_start = lax.axis_index("dp") * col_width
    summed = lax.psum(partial_terms, "section") * scale
    features = lax.all_gather(summed, "dp", axis=0, tiled=True)
    row_block = lax.dynamic_slice_in_dim(features, row_start, row_width, 1)
    col_block = lax.dynamic_slice_in_dim(features, col_start, col_width, 1)
    outer = jnp.dot(row_block.T, col_block, precision=lax.Precision.HIGHEST)
    return earlier_gram + outer / total_examples


def solution(mesh):
    return jax.shard_map(
        per_device,
        mesh=mesh,
        in_specs=(
            P("section", "dp", None, None),
            P("section", "dp", None, None),
            P("section", None, None, None),
            P("section", None, None, None),
            P("section", "dp"),
        ),
        out_specs=P("section", "dp"),
        check_vma=False,
    )
```

profile of v0, /device:TPU:0, one launch (start us, length us, event | category | flops | bytes accessed | tf_op | source)
XLA Modules:
  0.0 136.9 jit_solution(12887768697109643629)
XLA Ops:
  6.5 0.0 copy-start
  6.5 0.0 all-reduce.2.cloned.1.call-start
  6.5 4.8 %fusion.13 = bf16[2,8,64,64]{3,2,0,1:T(8,128)(2,1)S(1)} fusion(bf16[1,8,64,4096]{3,2,1,0:T(8,128)(2,1)} %param.6, bf16[1,2,64,4096]{3,2,1,0:T(8,128)(2,1)} %param.8), kind=kOutput, calls=%fused_computation.8 | convolution fusion | flops 536936448 | bytes 5373952 | tf_op jit(solution)/shard_map/pkd,etd->pekt/dot_general | solution.py:19
  11.3 0.0 copy-done
  11.3 3.6 %convolution_bitcast_fusion = f32[1,8,64,128]{3,2,1,0:T(8,128)S(1)} fusion(bf16[2,8,64,64]{3,2,0,1:T(8,128)(2,1)S(1)} %fusion.13, bf16[1,8,64,4096]{3,2,1,0:T(8,128)(2,1)} %param.5, bf16[1,2,4096,128]{3,2,1,0:T(8,128)(2,1)S(1)} %copy-done), kind=kOutput, calls=%fused_computation.9 | convolution fusion | flops 1090650112 | bytes 6684672 | tf_op jit(solution)/shard_map/pekt,petm->ekm/dot_general | solution.py:22
  15.0 0.9 copy.11
  15.8 0.0 all-reduce.2.cloned.1.call-update
  15.9 92.6 %all-reduce.2.cloned.1.call-done = f32[8,8192]{1,0:T(8,128)} async-done(((f32[8,8192]{1,0:T(8,128)}), f32[8,8192]{1,0:T(8,128)}) %all-reduce.2.cloned.1.call-update) | async-done | bytes 262160 | tf_op jit(solution)/shard_map/psum | solution.py:35
  108.5 1.0 broadcast_multiply_fusion
  109.4 9.3 %all_gather.3 = f32[16,8192]{1,0:T(8,128)S(1)} all-gather(f32[8,8192]{1,0:T(8,128)S(1)} %broadcast_multiply_fusion), channel_id=1, replica_groups=mesh['section'=16,'dp'=2] {'dp'}, dimensions={0}, use_global_device_ids=true | all-gather | bytes 786432 | tf_op jit(solution)/shard_map/all_gather | solution.py:36
  118.8 11.3 %multiply_add_fusion = f32[512,4096]{1,0:T(8,128)} fusion(f32[512,4096]{1,0:T(8,128)} %param.9, f32[16,8192]{1,0:T(8,128)S(1)} %all_gather.3, s32[]{:T(128)S(6)} %select_n.7, s32[]{:T(128)S(6)} %select_n.6), kind=kOutput, calls=%fused_computation | convolution fusion | flops 406847488 | bytes 17072136 | tf_op jit(solution)/shard_map/dot_general | solution.py:39
Async XLA Ops:
  6.5 4.8 %copy-start = (bf16[1,2,4096,128]{3,2,1,0:T(8,128)(2,1)S(1)}, bf16[1,2,4096,128]{3,2,1,0:T(8,128)(2,1)}, u32[]{:S(2)}) copy-start(bf16[1,2,4096,128]{3,2,1,0:T(8,128)(2,1)} %param.7) | copy-start | bytes 6291460
  6.5 101.9 %all-reduce.2.cloned.1.call-start = ((), (), s32[]{:S(2)}) async-start(), calls=%async_computation | async-start | bytes 524288 | tf_op jit(solution)/shard_map/psum | solution.py:35
Sparse Core Ops, SparseCore 0:
  16.0 92.4 all-reduce.1
where the time goes:
time: 137 us
  waiting for transfers between devices  92.6 us (68%)
  matrix products  19.8 us (14%)
  between operations  13.4 us (10%)
  blocking collectives  9.31 us (7%)
    psum x1, waiting for transfers between devices, per_device(): summed = lax.psum(partial_terms, 'section') * scale  92.6 us
    dot_general x1, matrix products, per_device(): outer = jnp.dot(row_block.T, col_block, precision=lax.Precision.HIGHEST)  11.3 us
    all_gather x1, blocking collectives, per_device(): features = lax.all_gather(summed, 'dp', axis=0, tiled=True)  9.31 us
    dot_general x1, matrix products, per_device(): jnp.einsum('pkd,etd->pekt', layer_out, layer_grad, preferred_element_type...  4.78 us
    dot_general x1, matrix products, per_device(): jnp.einsum('pekt,petm->ekm', low_out, low_in, preferred_element_type=jnp....  3.63 us
  transfers between devices with their start and end apart: 1, of which 1 were waited for; matrix products, arithmetic and copies ran while one was open for 0% of the time, Pallas kernels for 0%

commit v1 on v0

--- a/solution.py
+++ b/solution.py
@@ -32,7 +32,11 @@
     col_width = earlier_gram.shape[1]
     row_start = lax.axis_index("section") * row_width
     col_start = lax.axis_index("dp") * col_width
-    summed = lax.psum(partial_terms, "section") * scale
+
+    def words_shape(incoming_x):
+        return jnp.sum(lax.all_gather(incoming_x, "section"), 0)
+
+    summed = words_shape(partial_terms) * scale
     features = lax.all_gather(summed, "dp", axis=0, tiled=True)
     row_block = lax.dynamic_slice_in_dim(features, row_start, row_width, 1)
     col_block = lax.dynamic_slice_in_dim(features, col_start, col_width, 1)

time: 137 us -> 99 us (0.72)
  waiting for transfers between devices: 92.6 us -> 53.3 us
  other arithmetic: 0.97 us -> 2.43 us
    psum x1 -> x0, waiting for transfers between devices: 92.6 us -> none  [per_device(): summed = lax.psum(partial_terms, 'section') * scale]
    all_gather x0 -> x1, waiting for transfers between devices: none -> 53.3 us  [words_shape(): return jnp.sum(lax.all_gather(incoming_x, 'section'), 0)]
    reduce_sum x0 -> x1, other arithmetic: none -> 2.4 us  [words_shape(): return jnp.sum(lax.all_gather(incoming_x, 'section'), 0)]
where the time goes in v1:
time: 99 us; the launch traced here: 98.8 us
  waiting for transfers between devices  53.3 us (54%)
  matrix products  19.8 us (20%)
  between operations  13.4 us (14%)
  blocking collectives  9.12 us (9%)
  other arithmetic  2.43 us (2%)
    all_gather x1, waiting for transfers between devices, words_shape(): return jnp.sum(lax.all_gather(incoming_x, 'section'), 0)  53.3 us
    dot_general x1, matrix products, per_device(): outer = jnp.dot(row_block.T, col_block, precision=lax.Precision.HIGHEST)  11.3 us
    all_gather x1, blocking collectives, per_device(): features = lax.all_gather(summed, 'dp', axis=0, tiled=True)  9.12 us
    dot_general x1, matrix products, per_device(): jnp.einsum('pkd,etd->pekt', layer_out, layer_grad, preferred_element_type...  4.78 us
    dot_general x1, matrix products, per_device(): jnp.einsum('pekt,petm->ekm', low_out, low_in, preferred_element_type=jnp....  3.63 us
    reduce_sum x1, other arithmetic, words_shape(): return jnp.sum(lax.all_gather(incoming_x, 'section'), 0)  2.4 us
  transfers between devices with their start and end apart: 1, of which 1 were waited for; matrix products, arithmetic and copies ran while one was open for 0% of the time, Pallas kernels for 0%

profile of v1, /device:TPU:0, one launch (start us, length us, event | category | flops | bytes accessed | tf_op | source)
XLA Modules:
  0.0 98.8 jit_solution(15637832693083162753)
XLA Ops:
  6.5 0.0 copy-start
  6.5 0.0 all-gather.2.cloned.1.call-start
  6.5 4.8 %fusion.13 = bf16[2,8,64,64]{3,2,0,1:T(8,128)(2,1)S(1)} fusion(bf16[1,8,64,4096]{3,2,1,0:T(8,128)(2,1)} %param.6, bf16[1,2,64,4096]{3,2,1,0:T(8,128)(2,1)} %param.8), kind=kOutput, calls=%fused_computation.8 | convolution fusion | flops 536936448 | bytes 5373952 | tf_op jit(solution)/shard_map/pkd,etd->pekt/dot_general | solution.py:19
  11.3 0.0 copy-done
  11.3 3.6 %convolution_bitcast_fusion = f32[8,64,128]{2,1,0:T(8,128)S(1)} fusion(bf16[2,8,64,64]{3,2,0,1:T(8,128)(2,1)S(1)} %fusion.13, bf16[1,8,64,4096]{3,2,1,0:T(8,128)(2,1)} %param.5, bf16[1,2,4096,128]{3,2,1,0:T(8,128)(2,1)S(1)} %copy-done), kind=kOutput, calls=%fused_computation.9 | convolution fusion | flops 1090650112 | bytes 6684672 | tf_op jit(solution)/shard_map/pekt,petm->ekm/dot_general | solution.py:22
  15.0 0.8 all_gather_reshape.3
  15.7 0.0 all-gather.2.cloned.1.call-update
  15.8 53.3 %all-gather.2.cloned.1.call-done = f32[16,8,8192]{2,1,0:T(8,128)} async-done(((f32[1,8,8192]{2,1,0:T(8,128)}), f32[16,8,8192]{2,1,0:T(8,128)}) %all-gather.2.cloned.1.call-update) | async-done | bytes 4194320 | tf_op jit(solution)/shard_map/all_gather | solution.py:37
  69.0 2.4 %reduce_sum.9 = f32[8,8192]{1,0:T(8,128)S(1)} reduce(f32[16,8,8192]{2,1,0:T(8,128)} %all-gather.2.cloned.1.call-done, f32[]{:T(128)} %constant.9.clone.1), dimensions={0}, to_apply=%region_0.0 | reduce | flops 983040 | bytes 4456452 | tf_op jit(solution)/shard_map/reduce_sum | solution.py:37
  71.5 9.1 %all_gather.7 = f32[16,8192]{1,0:T(8,128)S(1)} all-gather(f32[8,8192]{1,0:T(8,128)S(1)} %broadcast_multiply_fusion), channel_id=1, replica_groups=mesh['section'=16,'dp'=2] {'dp'}, dimensions={0}, use_global_device_ids=true | all-gather | bytes 786432 | tf_op jit(solution)/shard_map/all_gather | solution.py:40
  80.6 11.3 %multiply_add_fusion = f32[512,4096]{1,0:T(8,128)} fusion(f32[512,4096]{1,0:T(8,128)} %param.9, f32[16,8192]{1,0:T(8,128)S(1)} %all_gather.7, s32[]{:T(128)S(6)} %select_n.7, s32[]{:T(128)S(6)} %select_n.6), kind=kOutput, calls=%fused_computation | convolution fusion | flops 406847488 | bytes 17072136 | tf_op jit(solution)/shard_map/dot_general | solution.py:43
  (1 shorter events, 0.0 us)
Async XLA Ops:
  6.5 4.8 %copy-start = (bf16[1,2,4096,128]{3,2,1,0:T(8,128)(2,1)S(1)}, bf16[1,2,4096,128]{3,2,1,0:T(8,128)(2,1)}, u32[]{:S(2)}) copy-start(bf16[1,2,4096,128]{3,2,1,0:T(8,128)(2,1)} %param.7) | copy-start | bytes 6291460
  6.5 62.5 %all-gather.2.cloned.1.call-start = ((), (), s32[]{:S(2)}) async-start(), calls=%async_computation | async-start | bytes 4456448 | tf_op jit(solution)/shard_map/all_gather | solution.py:37
Sparse Core Ops, SparseCore 0:
  15.9 53.0 all-gather.1
